TPU v7x, 32 devices: a whole 2x2x4 slice. The times are simulated.
32 devices in a mesh: dp: 16 (over z, y, core), tensor: 2 (over x).
Axes of the slice: x: 2, y: 2, z: 4, core: 2. Of those that a mesh axis runs over, the one named last changes fastest.
Arguments:
- block_input: bfloat16 [160, 197, 768], P('dp'), may hold values from -6 to 6
- image_counts: int32 [16], P('dp'), may hold values from 1 to 10, 88 in all
- first_norm_gain: float32 [768], replicated, may hold values from 0.1 to 1.9
- first_norm_bias: float32 [768], replicated, may hold values from -3 to 3
- w_qkv: bfloat16 [3, 768, 768], P(None, None, 'tensor'), may hold values from -8 to 8
- qv_bias: float32 [2, 768], P(None, 'tensor'), may hold values from -3 to 3
- w_out: bfloat16 [768, 768], P('tensor'), may hold values from -0.75 to 0.75
- b_out: float32 [768], replicated, may hold values from -3 to 3
- second_norm_gain: float32 [768], replicated, may hold values from 0.1 to 1.9
- second_norm_bias: float32 [768], replicated, may hold values from -3 to 3
- w_fc1: bfloat16 [768, 3072], P(None, 'tensor'), may hold values from -0.21875 to 0.21875
- b_fc1: float32 [3072], P('tensor'), may hold values from -3 to 3
- w_fc2: bfloat16 [3072, 768], P('tensor'), may hold values from -0.109375 to 0.109375
- b_fc2: float32 [768], replicated, may hold values from -3 to 3
- cotangent: bfloat16 [160, 197, 768], P('dp'), may hold values from -6 to 6
Outputs:
- block_out: bfloat16 [160, 197, 768], P('dp')
- gradient_of_input: bfloat16 [160, 197, 768], P('dp')
- first_norm_gain_gradient: float32 [768], replicated
- grad_ln1_bias: float32 [768], replicated
- grad_w_qkv: float32 [3, 768, 768], P(None, None, 'tensor')
- grad_qv_bias: float32 [2, 768], P(None, 'tensor')
- grad_w_out: float32 [768, 768], P('tensor')
- grad_b_out: float32 [768], replicated
- second_norm_gain_gradient: float32 [768], replicated
- grad_ln2_bias: float32 [768], replicated
- grad_w_fc1: float32 [768, 3072], P(None, 'tensor')
- grad_b_fc1: float32 [3072], P('tensor')
- grad_w_fc2: float32 [3072, 768], P('tensor')
- grad_b_fc2: float32 [768], replicated
All inputs are finite; a program needn't handle non-finite values. No bound on the sum of `image_counts` on one device may be relied on, other than what follows from the above.
Results may differ from a plain program's by a relative error of at most 0.012.
The roundings to bfloat16 on the way count: a program that leaves them out, or rounds other values in their place, can miss the bound.
Values sent between devices are 32-bit elements; how exact they have to be, the bound alone decides.
No kernel may reach another device: no remote copies, remote signals or barrier semaphores. Data moves between devices by JAX's collectives and lax.ppermute only.
A program may use at most 256 MiB of HBM per device.

v0:
```python
import jax
import jax.numpy as jnp
from jax import lax
from jax.sharding import PartitionSpec as P

HD = 64
EPSILON = 1e-06
INV_ROOT2 = 0.7071067811865476
INV_ROOT2PI = 0.3989422804014327


def apply_layer_norm(values, norm_gain, norm_bias):
    center = jnp.mean(values, -1, keepdims=True)
    shifted = values - center
    spread = jnp.mean(shifted * shifted, -1, keepdims=True)
    inv_std = lax.rsqrt(spread + EPSILON)
    normed = shifted * inv_std
    return (normed * norm_gain + norm_bias, normed, inv_std)


def norm_backward_pass(grad_normed, normed, inv_std, norm_gain):
    scaled = grad_normed * norm_gain
    first = jnp.mean(scaled, -1, keepdims=True)
    second = jnp.mean(scaled * normed, -1, keepdims=True)
    return inv_std * (scaled - first - normed * second)


def gelu_value(pre_act):
    return 0.5 * pre_act * (1.0 + lax.erf(pre_act * INV_ROOT2))


def gelu_slope(pre_act):
    return (
        0.5 * (1.0 + lax.erf(pre_act * INV_ROOT2))
        + pre_act * jnp.exp(-0.5 * pre_act * pre_act) * INV_ROOT2PI
    )


def head_scores(queries, keys_all, scale):
    return (
        jnp.einsum("ishd,ithd->ihst", queries, keys_all, preferred_element_type=jnp.float32) * scale
    )


def shards(
    block_input,
    image_counts,
    first_norm_gain,
    first_norm_bias,
    w_qkv,
    qv_bias,
    w_out,
    b_out,
    second_norm_gain,
    second_norm_bias,
    w_fc1,
    b_fc1,
    w_fc2,
    b_fc2,
    cotangent,
):
    float_thirtytwo = jnp.float32
    bfloat_sixteen = jnp.bfloat16
    image_batch, sequence_length, model_width = block_input.shape
    total_rows = image_batch * sequence_length
    local_heads = w_qkv.shape[2] // HD
    local_width = local_heads * HD
    scale = HD ** (-0.5)
    shape4 = (image_batch, sequence_length, local_heads, HD)
    live_rows = (jnp.arange(total_rows, dtype=jnp.int32) // sequence_length < image_counts[0])[
        :, None
    ]
    input_tokens = block_input.reshape(total_rows, model_width).astype(float_thirtytwo)
    first_normed_tokens, first_centered_scaled, first_inverse_deviation = apply_layer_norm(
        input_tokens, first_norm_gain, first_norm_bias
    )
    normed_one_b = first_normed_tokens.astype(bfloat_sixteen)
    projected = jnp.einsum(
        "nd,cde->cne", normed_one_b, w_qkv, preferred_element_type=float_thirtytwo
    )
    queries = (projected[0] + qv_bias[0]).astype(bfloat_sixteen).reshape(shape4)
    keys_all = projected[1].astype(bfloat_sixteen).reshape(shape4)
    values_all = (projected[2] + qv_bias[1]).astype(bfloat_sixteen).reshape(shape4)
    scores = head_scores(queries, keys_all, scale)
    log_total = jax.nn.logsumexp(scores, axis=-1)
    probs = jnp.exp(scores - log_total[..., None]).astype(bfloat_sixteen)
    context = (
        jnp.einsum("ihst,ithd->ishd", probs, values_all, preferred_element_type=float_thirtytwo)
        .astype(bfloat_sixteen)
        .reshape(total_rows, local_width)
    )
    attn_part = jnp.dot(context, w_out, preferred_element_type=float_thirtytwo)
    attn_full = lax.psum(attn_part, "tensor")
    residual_stream = input_tokens + (attn_full + b_out)
    second_normed_tokens, second_centered_scaled, second_inverse_deviation = apply_layer_norm(
        residual_stream, second_norm_gain, second_norm_bias
    )
    normed_two_b = second_normed_tokens.astype(bfloat_sixteen)
    pre_act = jnp.dot(normed_two_b, w_fc1, preferred_element_type=float_thirtytwo) + b_fc1
    activated = gelu_value(pre_act).astype(bfloat_sixteen)
    mlp_part = jnp.dot(activated, w_fc2, preferred_element_type=float_thirtytwo)
    mlp_full = lax.psum(mlp_part, "tensor")
    outputs = residual_stream + (mlp_full + b_fc2)
    block_out = (
        jnp.where(live_rows, outputs, 0.0)
        .astype(bfloat_sixteen)
        .reshape(image_batch, sequence_length, model_width)
    )
    output_gradient = jnp.where(
        live_rows, cotangent.reshape(total_rows, model_width), jnp.zeros((), bfloat_sixteen)
    )
    grad_w_fc2 = jnp.einsum(
        "nf,nd->fd", activated, output_gradient, preferred_element_type=float_thirtytwo
    )
    grad_b_fc2 = jnp.sum(output_gradient.astype(float_thirtytwo), axis=0)
    grad_act = jnp.einsum(
        "nd,fd->nf", output_gradient, w_fc2, preferred_element_type=float_thirtytwo
    )
    grad_pre = (grad_act * gelu_slope(pre_act)).astype(bfloat_sixteen)
    grad_w_fc1 = jnp.einsum(
        "nd,nf->df", normed_two_b, grad_pre, preferred_element_type=float_thirtytwo
    )
    grad_b_fc1 = jnp.sum(grad_pre.astype(float_thirtytwo), axis=0)
    norm_two_part = jnp.einsum("nf,df->nd", grad_pre, w_fc1, preferred_element_type=float_thirtytwo)
    second_normed_gradient = lax.psum(norm_two_part, "tensor")
    second_norm_gain_gradient = jnp.sum(second_normed_gradient * second_centered_scaled, axis=0)
    grad_ln2_bias = jnp.sum(second_normed_gradient, axis=0)
    residual_gradient = output_gradient.astype(float_thirtytwo) + norm_backward_pass(
        second_normed_gradient, second_centered_scaled, second_inverse_deviation, second_norm_gain
    )
    grad_resid_b = residual_gradient.astype(bfloat_sixteen)
    grad_w_out = jnp.einsum(
        "ne,nd->ed", context, grad_resid_b, preferred_element_type=float_thirtytwo
    )
    grad_b_out = jnp.sum(residual_gradient, axis=0)
    grad_context = (
        jnp.einsum("nd,ed->ne", grad_resid_b, w_out, preferred_element_type=float_thirtytwo)
        .astype(bfloat_sixteen)
        .reshape(shape4)
    )
    probs_full = jnp.exp(head_scores(queries, keys_all, scale) - log_total[..., None])
    probs_again = probs_full.astype(bfloat_sixteen)
    grad_values = jnp.einsum(
        "ihst,ishd->ithd", probs_again, grad_context, preferred_element_type=float_thirtytwo
    ).astype(bfloat_sixteen)
    grad_probs = jnp.einsum(
        "ishd,ithd->ihst", grad_context, values_all, preferred_element_type=float_thirtytwo
    )
    row_dot = jnp.sum(probs_full * grad_probs, axis=-1, keepdims=True)
    grad_scores = (probs_full * (grad_probs - row_dot)).astype(bfloat_sixteen)
    grad_queries = (
        jnp.einsum("ihst,ithd->ishd", grad_scores, keys_all, preferred_element_type=float_thirtytwo)
        * scale
    ).astype(bfloat_sixteen)
    grad_keys = (
        jnp.einsum("ihst,ishd->ithd", grad_scores, queries, preferred_element_type=float_thirtytwo)
        * scale
    ).astype(bfloat_sixteen)
    grad_proj = jnp.stack([grad_queries, grad_keys, grad_values]).reshape(
        3, total_rows, local_width
    )
    grad_w_qkv = jnp.einsum(
        "nd,cne->cde", normed_one_b, grad_proj, preferred_element_type=float_thirtytwo
    )
    grad_qv_bias = jnp.stack(
        [
            jnp.sum(grad_proj[0].astype(float_thirtytwo), axis=0),
            jnp.sum(grad_proj[2].astype(float_thirtytwo), axis=0),
        ]
    )
    norm_one_part = jnp.einsum(
        "cne,cde->nd", grad_proj, w_qkv, preferred_element_type=float_thirtytwo
    )
    first_normed_gradient = lax.psum(norm_one_part, "tensor")
    first_norm_gain_gradient = jnp.sum(first_normed_gradient * first_centered_scaled, axis=0)
    grad_ln1_bias = jnp.sum(first_normed_gradient, axis=0)
    gradient_of_input = (
        (
            residual_gradient
            + norm_backward_pass(
                first_normed_gradient,
                first_centered_scaled,
                first_inverse_deviation,
                first_norm_gain,
            )
        )
        .astype(bfloat_sixteen)
        .reshape(image_batch, sequence_length, model_width)
    )
    summed = lax.psum(
        (
            first_norm_gain_gradient,
            grad_ln1_bias,
            grad_w_qkv,
            grad_qv_bias,
            grad_w_out,
            grad_b_out,
            second_norm_gain_gradient,
            grad_ln2_bias,
            grad_w_fc1,
            grad_b_fc1,
            grad_w_fc2,
            grad_b_fc2,
        ),
        "dp",
    )
    first_norm_gain_gradient, grad_ln1_bias, grad_w_qkv, grad_qv_bias, grad_w_out, grad_b_out = (
        summed[0],
        summed[1],
        summed[2],
        summed[3],
        summed[4],
        summed[5],
    )
    second_norm_gain_gradient, grad_ln2_bias, grad_w_fc1, grad_b_fc1, grad_w_fc2, grad_b_fc2 = (
        summed[6],
        summed[7],
        summed[8],
        summed[9],
        summed[10],
        summed[11],
    )
    return (
        block_out,
        gradient_of_input,
        first_norm_gain_gradient,
        grad_ln1_bias,
        grad_w_qkv,
        grad_qv_bias,
        grad_w_out,
        grad_b_out,
        second_norm_gain_gradient,
        grad_ln2_bias,
        grad_w_fc1,
        grad_b_fc1,
        grad_w_fc2,
        grad_b_fc2,
    )


def solution(mesh):
    in_specs = (
        P("dp", None, None),
        P("dp"),
        P(),
        P(),
        P(None, None, "tensor"),
        P(None, "tensor"),
        P("tensor", None),
        P(),
        P(),
        P(),
        P(None, "tensor"),
        P("tensor"),
        P("tensor", None),
        P(),
        P("dp", None, None),
    )
    out_specs = (
        P("dp", None, None),
        P("dp", None, None),
        P(),
        P(),
        P(None, None, "tensor"),
        P(None, "tensor"),
        P("tensor", None),
        P(),
        P(),
        P(),
        P(None, "tensor"),
        P("tensor"),
        P("tensor", None),
        P(),
    )
    return jax.shard_map(shards, mesh=mesh, in_specs=in_specs, out_specs=out_specs, check_vma=False)
```

profile of v0, /device:TPU:0, one launch (start us, length us, event | category | flops | bytes accessed | tf_op | source)
XLA Modules:
  0.0 1190.0 jit_solution(15098997224716500326)
XLA Ops:
  7.3 6.9 reshape.188
  14.2 2.4 convert_reduce_fusion.4
  16.5 2.9 multiply_reduce_fusion.2
  19.7 7.4 convolution_bitcast_fusion
  27.2 3.0 fusion.36
  31.5 3.5 copy.41
  35.0 8.1 squeeze.14
  43.2 5.7 reshape.194
  48.9 5.6 copy.44
  54.5 3.7 add_convert_fusion
  58.3 2.6 multiply_reduce_fusion.1
  61.0 2.9 exponential_reduce_fusion
  65.3 3.5 copy.40
  68.9 8.1 squeeze.13
  77.0 3.1 add_convert_fusion.1
  80.2 8.9 convert_bitcast_fusion.1
  89.1 3.0 copy.47
  92.1 5.9 reshape.183
  98.0 5.7 fusion.37
  104.5 4.0 reshape.185
  108.5 146.6 %all-reduce.8.cloned.1.call-done = f32[1970,768]{1,0:T(8,128)} async-done(((f32[1970,768]{1,0:T(8,128)}), f32[1970,768]{1,0:T(8,128)}) %all-reduce.8.cloned.1.call-update) | async-done | bytes 6051856 | tf_op jit(solution)/shard_map/psum | solution.py:93
  255.1 5.2 fusion.35
  261.3 8.0 multiply_convert_fusion.1
  269.4 9.3 convert_reduce_fusion
  278.7 2.5 copy-done.36
  281.2 6.8 fusion.39
  288.1 10.1 fusion.29
  298.2 8.9 fusion.32
  307.1 130.0 %all-reduce.10.cloned.1.call-done = f32[1970,768]{1,0:T(8,128)} async-done(((f32[1970,768]{1,0:T(8,128)}), f32[1970,768]{1,0:T(8,128)}) %all-reduce.10.cloned.1.call-update) | async-done | bytes 6051856 | tf_op jit(solution)/shard_map/psum | solution.py:125
  437.2 6.0 multiply_reduce_fusion.3
  444.3 5.8 fusion.34
  450.1 3.0 fusion.10
  453.1 1.8 convolution_convert_fusion
  454.9 4.1 reshape.195
  459.0 4.9 copy.49
  464.0 8.5 convert_reduce_fusion.2
  472.5 12.1 %multiply_reduce_fusion = (f32[10,6,197]{2,1,0:T(8,128)S(1)}, f32[10,6,197,197]{2,3,1,0:T(8,128)}) fusion(f32[10,6,197,197]{2,3,1,0:T(8,128)} %copy-done.2, f32[10,6,197]{2,1,0:T(8,128)S(1)} %log_add_fusion, bf16[10,197,6,64]{1,3,2,0:T(8,128)(2,1)S(1)} %copy.49, bf16[10,197,6,64]{1,0,3,2:T(8,128)(2,1)} %copy-done.11), kind=kOutput, calls=%fused_computation.2 | convolution fusion | flops 307355456 | bytes 21748800 | tf_op jit(solution)/shard_map/ishd,ithd->ihst/dot_general | solution.py:146
  484.6 6.5 multiply_convert_fusion
  491.1 5.1 fusion.9
  496.2 2.6 convert_reduce_fusion.3
  498.9 5.8 copy.70
  504.6 6.0 reshape.193
  510.6 5.9 copy.69
  516.5 6.0 reshape.192
  522.5 4.3 copy.68
  526.9 6.1 reshape.191
  532.9 1.5 constant_dynamic-update-slice_fusion.2
  534.5 1.7 constant_dynamic-update-slice_fusion.1
  536.5 2.1 copy-done.18
  538.6 9.1 convolution_bitcast_fusion.2
  547.8 11.2 fusion.38
  559.0 6.2 convolution_bitcast_fusion.1
  565.3 2.3 convert_reduce_fusion.1
  567.7 236.9 %all-reduce.12.cloned.1.call-done = (f32[3,768,384]{1,2,0:T(8,128)}, f32[384,768]{1,0:T(8,128)}, f32[768,1536]{1,0:T(8,128)}, f32[1536,768]{1,0:T(8,128)}) async-done(((f32[3,768,384]{1,2,0:T(8,128)}, f32[384,768]{1,0:T(8,128)}, f32[768,1536]{1,0:T(8,128)}, f32[1536,768]{1,0:T(8,128)}), (f32[3,768,384]{1,2,0:T(8,128)}, f32[384,768]{1,0:T(8,128)}, f32[768,1536]{1,0:T(8,128)}, ...) | async-done | bytes 14155792 | tf_op jit(solution)/shard_map/psum | solution.py:190
  804.6 5.2 copy.63
  809.7 275.8 %all-reduce.14.cloned.1.call-done = (f32[1970,768]{1,0:T(8,128)}, f32[1970,768]{1,0:T(8,128)}) async-done(((f32[1970,768]{1,0:T(8,128)}, f32[1970,768]{1,0:T(8,128)}), (f32[1970,768]{1,0:T(8,128)}, f32[1970,768]{1,0:T(8,128)})) %all-reduce.14.cloned.1.call-update) | async-done | bytes 12103696 | tf_op jit(solution)/shard_map/psum | solution.py:102
  1085.6 5.9 multiply_reduce_fusion.4
  1091.8 6.7 add_convert_fusion.2
  1098.5 4.1 reshape.187
  1102.6 6.6 select_convert_fusion
  1109.1 4.1 reshape.184
  1113.3 61.7 %all-reduce = (f32[768]{0:T(1024)}, f32[768]{0:T(1024)}, f32[2,384]{1,0:T(2,128)}, f32[768]{0:T(1024)}, f32[768]{0:T(1024)}, /*index=5*/f32[768]{0:T(1024)}, f32[1536]{0:T(1024)}, f32[768]{0:T(1024)}) all-reduce(f32[768]{0:T(1024)S(1)} %get-tuple-element.44, ...), channel_id=1, replica_groups=mesh['dp'=16,'tensor'=2] {'dp'}, use_global_device_ids=true, to_apply=%region_16.17 | all-reduce | flops 6912 | bytes 55296 | tf_op jit(solution)/shard_map/psum | solution.py:190
  1176.0 5.0 copy.102
  1181.0 2.2 copy.103
  (117 shorter events, 7.3 us)
Async XLA Ops:
  7.2 254.1 %copy-start = (bf16[768,1536]{1,0:T(8,128)(2,1)S(1)}, bf16[768,1536]{1,0:T(8,128)(2,1)}, u32[]{:S(2)}) copy-start(bf16[768,1536]{1,0:T(8,128)(2,1)} %param.25) | copy-start | bytes 7077892
  7.2 12.5 %copy-start.24 = (f32[768]{0:T(1024)S(1)}, f32[768]{0:T(1024)}, u32[]{:S(2)}) copy-start(f32[768]{0:T(1024)} %param.17) | copy-start | bytes 9220
  7.2 12.5 %copy-start.34 = (f32[768]{0:T(1024)S(1)}, f32[768]{0:T(1024)}, u32[]{:S(2)}) copy-start(f32[768]{0:T(1024)} %param.18) | copy-start | bytes 9220
  7.2 247.9 %all-reduce.8.cloned.1.call-start = ((), (), s32[]{:S(2)}) async-start(), calls=%async_computation | async-start | bytes 12140544 | tf_op jit(solution)/shard_map/psum | solution.py:93
  19.5 7.6 copy-start.20
  19.7 7.5 copy-start.22
  35.0 8.1 copy-start.29
  54.5 3.7 copy-start.5
  58.3 2.6 copy-start.10
  60.9 4.3 copy-start.2
  80.1 8.9 copy-start.11
  89.0 9.0 copy-start.16
  103.7 151.4 %copy-start.27 = (f32[768]{0:T(1024)S(1)}, f32[768]{0:T(1024)}, u32[]{:S(2)}) copy-start(f32[768]{0:T(1024)} %param.22) | copy-start | bytes 9220
  103.8 333.4 %all-reduce.10.cloned.1.call-start = ((), (), s32[]{:S(2)}) async-start(), calls=%async_computation.1 | async-start | bytes 12140544 | tf_op jit(solution)/shard_map/psum | solution.py:125
  260.4 9.0 copy-start.3
  260.4 0.9 copy-start.26
  260.4 0.9 copy-start.32
  260.4 0.9 copy-start.33
  261.3 8.1 copy-start.13
  261.3 8.1 copy-start.30
  278.7 2.6 copy-start.36
  288.0 516.6 %all-reduce.12.cloned.1.call-start = ((), (), s32[]{:S(2)}) async-start(), calls=%async_computation.2 | async-start | bytes 28311552 | tf_op jit(solution)/shard_map/psum | solution.py:190
  288.1 10.2 copy-start.37
  437.2 6.2 copy-start.8
  437.2 7.1 copy-start.14
  444.3 5.8 copy-start.9
  450.1 3.0 copy-start.4
  463.9 20.6 %slice-start = ((s8[12288000]{0:T(1024)(128)(4,1)}), s8[4194304]{0:T(1024)(128)(4,1)S(1)}, s32[]{:S(2)}) async-start(s8[12288000]{0:T(1024)(128)(4,1)} %bitcast.49), calls=%async_computation.4 | async-start | bytes 8388608
  464.0 20.6 %slice-start.1 = ((s8[12288000]{0:T(1024)(128)(4,1)}), s8[4194304]{0:T(1024)(128)(4,1)S(1)}, s32[]{:S(2)}) async-start(s8[12288000]{0:T(1024)(128)(4,1)} %bitcast.49), calls=%async_computation.5 | async-start | bytes 8388608
  472.5 12.1 %slice-start.2 = ((s8[12288000]{0:T(1024)(128)(4,1)}), s8[3899392]{0:T(1024)(128)(4,1)S(1)}, s32[]{:S(2)}) async-start(s8[12288000]{0:T(1024)(128)(4,1)} %bitcast.49), calls=%async_computation.6 | async-start | bytes 7798784
  491.1 5.1 copy-start.6
  510.6 11.9 %copy-start.12 = (bf16[10,197,6,64]{1,3,2,0:T(8,128)(2,1)S(1)}, bf16[10,197,6,64]{1,3,2,0:T(8,128)(2,1)}, u32[]{:S(2)}) copy-start(bf16[10,197,6,64]{1,3,2,0:T(8,128)(2,1)} %get-tuple-element.81) | copy-start | bytes 4538884
  526.8 9.3 copy-start.15
  526.8 11.8 copy-start.21
  526.8 11.8 copy-start.23
  526.8 11.8 copy-start.25
  526.8 11.8 copy-start.35
  536.5 2.1 copy-start.18
  547.8 537.8 %all-reduce.14.cloned.1.call-start = ((), (), s32[]{:S(2)}) async-start(), calls=%async_computation.3 | async-start | bytes 24281088 | tf_op jit(solution)/shard_map/psum | solution.py:102
  547.8 11.2 copy-start.19
  547.8 11.2 copy-start.31
  1085.6 6.2 copy-start.7
  1098.5 4.1 copy-start.28
  1109.1 65.9 %copy-start.17 = (f32[384,768]{1,0:T(8,128)S(1)}, f32[384,768]{1,0:T(8,128)}, u32[]{:S(2)}) copy-start(f32[384,768]{1,0:T(8,128)} %get-tuple-element.92) | copy-start | bytes 3538948
  1113.3 67.8 %slice-start.3 = ((s8[4718592]{0:T(1024)(128)(4,1)}), s8[524288]{0:T(1024)(128)(4,1)S(1)}, s32[]{:S(2)}) async-start(s8[4718592]{0:T(1024)(128)(4,1)} %bitcast.51), calls=%async_computation.7 | async-start | bytes 1048576
  1176.0 5.0 slice-start.4
  1176.0 7.2 copy-start.1
Sparse Core Ops, SparseCore 0:
  103.9 151.1 all-reduce.7
  288.2 148.9 all-reduce.9
  547.9 256.6 all-reduce.11
  806.9 278.5 all-reduce.13
where the time goes:
time: 1200 us; the launch traced here: 1190 us
  waiting for transfers between devices  789 us (66%)
  local copies, waits for them, and re-layouts  135 us (11%)
  matrix products  127 us (11%)
  blocking collectives  61.7 us (5%)
  other arithmetic  61 us (5%)
  between operations  15.2 us (1%)
    psum x1, waiting for transfers between devices, shards(): mlp_full = lax.psum(mlp_part, 'tensor')  276 us
    psum x1, waiting for transfers between devices, shards(): lax.psum((first_norm_gain_gradient, grad_ln1_bias, grad_w_qkv, grad_qv_bi...  237 us
    psum x1, waiting for transfers between devices, shards(): attn_full = lax.psum(attn_part, 'tensor')  147 us
    psum x1, waiting for transfers between devices, shards(): second_normed_gradient = lax.psum(norm_two_part, 'tensor')  130 us
    psum x1, blocking collectives, shards(): lax.psum((first_norm_gain_gradient, grad_ln1_bias, grad_w_qkv, grad_qv_bi...  61.7 us
    another operation x7, local copies, waits for them, and re-layouts, shards(): jnp.stack([grad_queries, grad_keys, grad_values])  34.4 us
    unnamed x92, local copies, waits for them, and re-layouts  24.3 us
  transfers between devices with their start and end apart: 4, of which 4 were waited for; matrix products, arithmetic and copies ran while one was open for 4% of the time, Pallas kernels for 0%

commit v1 on v0

--- a/solution.py
+++ b/solution.py
@@ -90,7 +90,8 @@
         .reshape(total_rows, local_width)
     )
     attn_part = jnp.dot(context, w_out, preferred_element_type=float_thirtytwo)
-    attn_full = lax.psum(attn_part, "tensor")
+    theirs = lax.ppermute(attn_part, "tensor", [(0, 1), (1, 0)])
+    attn_full = attn_part + theirs
     residual_stream = input_tokens + (attn_full + b_out)
     second_normed_tokens, second_centered_scaled, second_inverse_deviation = apply_layer_norm(
         residual_stream, second_norm_gain, second_norm_bias

time: 1200 us -> 1190 us (level)
  waiting for transfers between devices: 789 us -> 770 us
    psum x1 -> x0, waiting for transfers between devices: 147 us -> none  [shards(): attn_full = lax.psum(attn_part, 'tensor')]
    ppermute x0 -> x1, waiting for transfers between devices: none -> 126 us  [shards(): theirs = lax.ppermute(attn_part, 'tensor', [(0, 1), (1, 0)])]
where the time goes in v1:
time: 1190 us; the launch traced here: 1180 us
  waiting for transfers between devices  770 us (65%)
  local copies, waits for them, and re-layouts  136 us (11%)
  matrix products  128 us (11%)
  other arithmetic  68.2 us (6%)
  blocking collectives  61.7 us (5%)
  between operations  15.1 us (1%)
    psum x1, waiting for transfers between devices, shards(): mlp_full = lax.psum(mlp_part, 'tensor')  276 us
    psum x1, waiting for transfers between devices, shards(): lax.psum((first_norm_gain_gradient, grad_ln1_bias, grad_w_qkv, grad_qv_bi...  237 us
    psum x1, waiting for transfers between devices, shards(): second_normed_gradient = lax.psum(norm_two_part, 'tensor')  131 us
    ppermute x1, waiting for transfers between devices, shards(): theirs = lax.ppermute(attn_part, 'tensor', [(0, 1), (1, 0)])  126 us
    psum x1, blocking collectives, shards(): lax.psum((first_norm_gain_gradient, grad_ln1_bias, grad_w_qkv, grad_qv_bi...  61.7 us
    another operation x7, local copies, waits for them, and re-layouts, shards(): jnp.stack([grad_queries, grad_keys, grad_values])  34.4 us
    unnamed x92, local copies, waits for them, and re-layouts  25 us
  transfers between devices with their start and end apart: 4, of which 4 were waited for; matrix products, arithmetic and copies ran while one was open for 4% of the time, Pallas kernels for 0%

profile of v1, /device:TPU:0, one launch (start us, length us, event | category | flops | bytes accessed | tf_op | source)
XLA Modules:
  0.0 1182.2 jit_solution(8866942042955673046)
XLA Ops:
  7.3 6.9 reshape.188
  14.2 2.4 convert_reduce_fusion.4
  16.5 2.9 multiply_reduce_fusion.2
  19.7 7.4 convolution_bitcast_fusion
  27.2 3.0 fusion.36
  31.5 3.5 copy.41
  35.0 8.1 squeeze.14
  43.2 5.7 reshape.194
  48.9 5.6 copy.44
  54.5 3.7 add_convert_fusion
  58.3 2.6 multiply_reduce_fusion.1
  61.0 2.9 exponential_reduce_fusion
  65.3 3.5 copy.40
  68.9 8.1 squeeze.13
  77.0 3.1 add_convert_fusion.1
  80.2 8.9 convert_bitcast_fusion.1
  89.1 3.0 copy.47
  92.1 5.9 reshape.183
  98.0 5.8 fusion.37
  103.8 3.0 collective-permute-start
  107.4 4.0 reshape.185
  111.5 126.4 %collective-permute-done = f32[1970,768]{1,0:T(8,128)} collective-permute-done((f32[1970,768]{1,0:T(8,128)}, f32[1970,768]{1,0:T(8,128)}, u32[]{:S(2)}, u32[]{:S(2)}) %collective-permute-start) | collective-permute-done | bytes 6051872 | tf_op jit(solution)/shard_map/ppermute | solution.py:93
  237.9 9.7 fusion.35
  247.6 3.6 multiply_reduce_fusion.7
  252.1 8.1 multiply_convert_fusion.1
  260.1 9.6 convert_reduce_fusion
  269.8 2.5 copy-done.36
  272.3 6.8 fusion.39
  279.2 10.1 fusion.29
  289.3 8.9 fusion.32
  298.2 131.0 %all-reduce.7.cloned.1.call-done = f32[1970,768]{1,0:T(8,128)} async-done(((f32[1970,768]{1,0:T(8,128)}), f32[1970,768]{1,0:T(8,128)}) %all-reduce.7.cloned.1.call-update) | async-done | bytes 6051856 | tf_op jit(solution)/shard_map/psum | solution.py:126
  429.2 6.0 multiply_reduce_fusion.3
  436.4 5.8 fusion.34
  442.2 3.0 fusion.10
  445.2 1.8 convolution_convert_fusion
  446.9 4.1 reshape.195
  451.1 4.9 copy.49
  456.0 8.5 convert_reduce_fusion.2
  464.5 12.1 %multiply_reduce_fusion = (f32[10,6,197]{2,1,0:T(8,128)S(1)}, f32[10,6,197,197]{2,3,1,0:T(8,128)}) fusion(f32[10,6,197,197]{2,3,1,0:T(8,128)} %copy-done.2, f32[10,6,197]{2,1,0:T(8,128)S(1)} %log_add_fusion, bf16[10,197,6,64]{1,3,2,0:T(8,128)(2,1)S(1)} %copy.49, bf16[10,197,6,64]{1,0,3,2:T(8,128)(2,1)} %copy-done.11), kind=kOutput, calls=%fused_computation.2 | convolution fusion | flops 307355456 | bytes 21748800 | tf_op jit(solution)/shard_map/ishd,ithd->ihst/dot_general | solution.py:147
  476.6 6.5 multiply_convert_fusion
  483.2 5.1 fusion.9
  488.3 2.6 convert_reduce_fusion.3
  490.9 5.8 copy.70
  496.7 6.0 reshape.193
  502.7 5.9 copy.69
  508.6 6.0 reshape.192
  514.6 4.3 copy.68
  518.9 6.1 reshape.191
  528.6 2.1 copy-done.18
  530.7 9.1 convolution_bitcast_fusion.2
  539.9 11.2 fusion.38
  551.1 6.2 convolution_bitcast_fusion.1
  557.3 2.3 convert_reduce_fusion.1
  559.8 236.9 %all-reduce.9.cloned.1.call-done = (f32[3,768,384]{1,2,0:T(8,128)}, f32[384,768]{1,0:T(8,128)}, f32[768,1536]{1,0:T(8,128)}, f32[1536,768]{1,0:T(8,128)}) async-done(((f32[3,768,384]{1,2,0:T(8,128)}, f32[384,768]{1,0:T(8,128)}, f32[768,1536]{1,0:T(8,128)}, f32[1536,768]{1,0:T(8,128)}), (f32[3,768,384]{1,2,0:T(8,128)}, f32[384,768]{1,0:T(8,128)}, f32[768,1536]{1,0:T(8,128)}, ...) | async-done | bytes 14155792 | tf_op jit(solution)/shard_map/psum | solution.py:191
  796.6 5.2 copy.63
  801.8 276.0 %all-reduce.11.cloned.1.call-done = (f32[1970,768]{1,0:T(8,128)}, f32[1970,768]{1,0:T(8,128)}) async-done(((f32[1970,768]{1,0:T(8,128)}, f32[1970,768]{1,0:T(8,128)}), (f32[1970,768]{1,0:T(8,128)}, f32[1970,768]{1,0:T(8,128)})) %all-reduce.11.cloned.1.call-update) | async-done | bytes 12103696 | tf_op jit(solution)/shard_map/psum | solution.py:103
  1077.8 5.9 multiply_reduce_fusion.4
  1084.0 6.7 add_convert_fusion.2
  1090.7 4.1 reshape.187
  1094.8 6.6 select_convert_fusion
  1101.3 4.1 reshape.184
  1105.5 61.7 %all-reduce = (f32[768]{0:T(1024)}, f32[768]{0:T(1024)}, f32[2,384]{1,0:T(2,128)}, f32[768]{0:T(1024)}, f32[768]{0:T(1024)}, /*index=5*/f32[768]{0:T(1024)}, f32[1536]{0:T(1024)}, f32[768]{0:T(1024)}) all-reduce(f32[768]{0:T(1024)S(1)} %get-tuple-element.44, ...), channel_id=1, replica_groups=mesh['dp'=16,'tensor'=2] {'dp'}, use_global_device_ids=true, to_apply=%region_15.16 | all-reduce | flops 6912 | bytes 55296 | tf_op jit(solution)/shard_map/psum | solution.py:191
  1168.2 5.0 copy.101
  1173.2 2.2 copy.102
  (116 shorter events, 10.4 us)
Async XLA Ops:
  7.2 244.1 %copy-start = (bf16[768,1536]{1,0:T(8,128)(2,1)S(1)}, bf16[768,1536]{1,0:T(8,128)(2,1)}, u32[]{:S(2)}) copy-start(bf16[768,1536]{1,0:T(8,128)(2,1)} %param.25) | copy-start | bytes 7077892
  7.2 12.5 %copy-start.24 = (f32[768]{0:T(1024)S(1)}, f32[768]{0:T(1024)}, u32[]{:S(2)}) copy-start(f32[768]{0:T(1024)} %param.17) | copy-start | bytes 9220
  7.2 12.5 %copy-start.34 = (f32[768]{0:T(1024)S(1)}, f32[768]{0:T(1024)}, u32[]{:S(2)}) copy-start(f32[768]{0:T(1024)} %param.18) | copy-start | bytes 9220
  7.2 422.0 %all-reduce.7.cloned.1.call-start = ((), (), s32[]{:S(2)}) async-start(), calls=%async_computation | async-start | bytes 12140544 | tf_op jit(solution)/shard_map/psum | solution.py:126
  19.5 7.6 copy-start.20
  19.7 7.5 copy-start.22
  35.0 8.1 copy-start.29
  54.5 3.7 copy-start.5
  58.3 2.6 copy-start.10
  60.9 4.3 copy-start.2
  80.1 8.9 copy-start.11
  89.0 9.0 copy-start.16
  98.0 139.9 %copy-start.27 = (f32[768]{0:T(1024)S(1)}, f32[768]{0:T(1024)}, u32[]{:S(2)}) copy-start(f32[768]{0:T(1024)} %param.22) | copy-start | bytes 9220
  103.8 134.1 %collective-permute-start = (f32[1970,768]{1,0:T(8,128)}, f32[1970,768]{1,0:T(8,128)}, u32[]{:S(2)}, u32[]{:S(2)}) collective-permute-start(f32[1970,768]{1,0:T(8,128)} %fusion.37), channel_id=1, source_target_pairs={{0,1},{1,0},{2,3},{3,2},{4,5},{5,4},{6,7},{7,6},{8,9},{9,8},{10,11... | collective-permute-start | bytes 18155528 | tf_op jit(solution)/shard_map/ppermute | solution.py:93
  247.5 4.5 copy-start.3
  247.5 4.5 copy-start.26
  247.5 4.5 copy-start.32
  247.5 4.5 copy-start.33
  252.0 8.1 copy-start.13
  252.0 8.1 copy-start.30
  269.8 2.6 copy-start.36
  279.1 517.5 %all-reduce.9.cloned.1.call-start = ((), (), s32[]{:S(2)}) async-start(), calls=%async_computation.1 | async-start | bytes 28311552 | tf_op jit(solution)/shard_map/psum | solution.py:191
  279.2 10.2 copy-start.37
  429.2 6.2 copy-start.8
  429.2 7.1 copy-start.14
  436.4 5.8 copy-start.9
  442.1 3.0 copy-start.4
  456.0 20.6 %slice-start = ((s8[12288000]{0:T(1024)(128)(4,1)}), s8[4194304]{0:T(1024)(128)(4,1)S(1)}, s32[]{:S(2)}) async-start(s8[12288000]{0:T(1024)(128)(4,1)} %bitcast.49), calls=%async_computation.3 | async-start | bytes 8388608
  456.0 20.6 %slice-start.1 = ((s8[12288000]{0:T(1024)(128)(4,1)}), s8[4194304]{0:T(1024)(128)(4,1)S(1)}, s32[]{:S(2)}) async-start(s8[12288000]{0:T(1024)(128)(4,1)} %bitcast.49), calls=%async_computation.4 | async-start | bytes 8388608
  464.5 12.1 %slice-start.2 = ((s8[12288000]{0:T(1024)(128)(4,1)}), s8[3899392]{0:T(1024)(128)(4,1)S(1)}, s32[]{:S(2)}) async-start(s8[12288000]{0:T(1024)(128)(4,1)} %bitcast.49), calls=%async_computation.5 | async-start | bytes 7798784
  483.2 5.1 copy-start.6
  502.7 11.9 %copy-start.12 = (bf16[10,197,6,64]{1,3,2,0:T(8,128)(2,1)S(1)}, bf16[10,197,6,64]{1,3,2,0:T(8,128)(2,1)}, u32[]{:S(2)}) copy-start(bf16[10,197,6,64]{1,3,2,0:T(8,128)(2,1)} %get-tuple-element.81) | copy-start | bytes 4538884
  518.9 9.3 copy-start.15
  518.9 11.8 copy-start.21
  518.9 11.8 copy-start.23
  518.9 11.8 copy-start.25
  518.9 11.8 copy-start.35
  528.6 2.1 copy-start.18
  539.8 538.0 %all-reduce.11.cloned.1.call-start = ((), (), s32[]{:S(2)}) async-start(), calls=%async_computation.2 | async-start | bytes 24281088 | tf_op jit(solution)/shard_map/psum | solution.py:103
  539.9 11.2 copy-start.19
  539.9 11.2 copy-start.31
  1077.8 6.2 copy-start.7
  1090.7 4.1 copy-start.28
  1101.3 65.9 %copy-start.17 = (f32[384,768]{1,0:T(8,128)S(1)}, f32[384,768]{1,0:T(8,128)}, u32[]{:S(2)}) copy-start(f32[384,768]{1,0:T(8,128)} %get-tuple-element.92) | copy-start | bytes 3538948
  1105.5 67.8 %slice-start.3 = ((s8[4718592]{0:T(1024)(128)(4,1)}), s8[524288]{0:T(1024)(128)(4,1)S(1)}, s32[]{:S(2)}) async-start(s8[4718592]{0:T(1024)(128)(4,1)} %bitcast.51), calls=%async_computation.6 | async-start | bytes 1048576
  1168.2 5.0 slice-start.4
  1168.2 7.2 copy-start.1
Sparse Core Ops, SparseCore 0:
  279.2 149.9 all-reduce.6
  539.9 256.6 all-reduce.8
  799.1 278.5 all-reduce.10
